TPU v7x, 256 devices: a whole 4x4x8 slice. The times are simulated.
256 devices in a mesh: row: 32 (over x, y, z_hi), rep: 8 (over z_lo, core).
Axes of the slice: x: 4, y: 4, z: 8 (z_hi: 2, z_lo: 4; z = z_hi * 4 + z_lo), core: 2. Of those that a mesh axis runs over, the one named last changes fastest.
Arguments:
- features: bfloat16 [65536, 256], P(('row', 'rep')), may hold values from -24 to 24
- weight: bfloat16 [256, 256], replicated, may hold values from -2 to 2
- degrees: int32 [65536], P(('row', 'rep')), may hold values from 1 to 16416, as said below
- cotangent: bfloat16 [65536, 256], P(('row', 'rep')), may hold values from -6 to 6
- tile_cols: int32 [4096, 16], P(('row', 'rep')), may hold values from 0 to 63, as said below
- list_len: int32 [4096], P(('row', 'rep')), may hold values from 1 to 16, as said below
- tiles: bfloat16 [4096, 16, 128, 128], P(('row', 'rep')), may hold values from 0 to 1, as said below
Outputs:
- activated: bfloat16 [65536, 256], P(('row', 'rep'))
- grad_x: bfloat16 [65536, 256], P(('row', 'rep'))
- grad_w: float32 [256, 256], P('row')
Inputs may be any that keep to these rules, and one draw needn't show every extreme that they name: `tile_cols`: within one list the 16 column tiles are distinct. `list_len`: on every device some list has exactly 16 live slots. `tiles`: entries are 0 or 1. `degrees`: each node's degree exceeds the number of ones in its row of A; some node has exactly the largest value.
All inputs are finite; a program needn't handle non-finite values.
Results may differ from a plain program's by a relative error of at most 0.006.
Values may be sent and summed in bfloat16 or wider, within the bound.
No kernel may reach another device: no remote copies, remote signals or barrier semaphores. Data moves between devices by JAX's collectives and lax.ppermute only.
A program may use at most 128 MiB of HBM per device.

v0:
```python
import math

import jax
import jax.numpy as jnp
from jax import lax
from jax.sharding import PartitionSpec as P


def on_device(features, weight, degrees, cotangent, tile_cols, list_len, tiles):
    node_rows, feat_width = features.shape
    tile_rows = tiles.shape[0]
    slot_count = tiles.shape[1]
    tile_size = tiles.shape[2]
    inv_root = 1.0 / jnp.sqrt(degrees.astype(jnp.float32))
    scaled_feats = (features.astype(jnp.float32) * inv_root[:, None]).astype(jnp.bfloat16)
    gathered = lax.all_gather(scaled_feats, "row", axis=0, tiled=True)
    section_tiles = gathered.reshape(-1, tile_size, feat_width)
    live_slots = (jnp.arange(slot_count)[None, :] < list_len[:, None]).astype(jnp.bfloat16)
    pattern = tiles * live_slots[:, :, None, None]
    picked = section_tiles[tile_cols]
    partial_value = jnp.einsum(
        "tkab,tkbf->taf", pattern, picked, preferred_element_type=jnp.float32
    )
    partial_value = partial_value.reshape(tile_rows * tile_size, feat_width)
    summed = lax.psum_scatter(partial_value, "rep", scatter_dimension=0, tiled=True)
    pooled = (summed * inv_root[:, None]).astype(jnp.bfloat16)
    preact = jnp.dot(pooled, weight, preferred_element_type=jnp.float32)
    activated = jax.nn.silu(preact).astype(jnp.bfloat16)
    sigmoid_val = jax.nn.sigmoid(preact)
    grad_pre = (
        cotangent.astype(jnp.float32) * sigmoid_val * (1.0 + preact * (1.0 - sigmoid_val))
    ).astype(jnp.bfloat16)
    weight_local = lax.dot_general(
        pooled, grad_pre, (((0,), (0,)), ((), ())), preferred_element_type=jnp.float32
    )
    back_rows = lax.dot_general(
        grad_pre, weight, (((1,), (1,)), ((), ())), preferred_element_type=jnp.float32
    )
    back_rows = (back_rows * inv_root[:, None]).astype(jnp.bfloat16)
    back_block = lax.all_gather(back_rows, "rep", axis=0, tiled=True).reshape(
        tile_rows, tile_size, feat_width
    )
    col_tiles = section_tiles.shape[0]

    def add_row(running, step_inputs):
        row_pattern, row_cols, row_back = step_inputs
        contrib = jnp.einsum(
            "kab,af->kbf", row_pattern, row_back, preferred_element_type=jnp.float32
        )
        return (running.at[row_cols].add(contrib), None)

    zero_sums = jnp.zeros((col_tiles, tile_size, feat_width), jnp.float32)
    col_sums, _ = lax.scan(add_row, zero_sums, (pattern, tile_cols, back_block))
    reduced_cols = lax.psum_scatter(
        col_sums.reshape(-1, feat_width), "row", scatter_dimension=0, tiled=True
    )
    node_total = node_rows * lax.axis_size("row") * lax.axis_size("rep")
    weight_norm = 1.0 / math.sqrt(node_total)
    rows_each = feat_width // lax.axis_size("row")
    weight_all = lax.psum(weight_local, ("row", "rep"))
    weight_rows = lax.dynamic_slice_in_dim(
        weight_all, lax.axis_index("row") * rows_each, rows_each, 0
    )
    grad_x = (reduced_cols * inv_root[:, None]).astype(jnp.bfloat16)
    return (activated, grad_x, weight_rows * weight_norm)


def solution(mesh):
    return jax.shard_map(
        on_device,
        mesh=mesh,
        in_specs=(
            P(("row", "rep"), None),
            P(),
            P(("row", "rep")),
            P(("row", "rep"), None),
            P(("row", "rep"), None),
            P(("row", "rep")),
            P(("row", "rep"), None, None, None),
        ),
        out_specs=(P(("row", "rep"), None), P(("row", "rep"), None), P("row", None)),
        check_vma=False,
    )
```

profile of v0, /device:TPU:0, one launch (start us, length us, event | category | flops | bytes accessed | tf_op | source)
XLA Modules:
  0.0 878.4 jit_solution(6991699257325208380)
XLA Ops:
  7.9 1.7 multiply_convert_fusion.4
  10.5 12.3 %copy.10 = bf16[16,16,128,128]{2,3,1,0:T(8,128)(2,1)} copy(bf16[16,16,128,128]{3,2,1,0:T(8,128)(2,1)} %param.15) | data formatting | bytes 16777216 | tf_op args[6]
  22.9 7.2 broadcast_multiply_fusion
  30.1 94.5 %all-gather.3.cloned.1.call-done = bf16[8192,256]{1,0:T(8,128)(2,1)} async-done(((bf16[256,256]{1,0:T(8,128)(2,1)}), bf16[8192,256]{1,0:T(8,128)(2,1)}) %all-gather.3.cloned.1.call-update) | async-done | bytes 4194320 | tf_op jit(solution)/shard_map/all_gather | solution.py:16
  124.7 12.0 %gather_fusion = bf16[256,128,256]{2,1,0:T(8,128)(2,1)} fusion(bf16[64,128,256]{2,1,0:T(8,128)(2,1)} %bitcast.39, s32[1024]{0:T(1024)S(1)} %pad_clamp_fusion), kind=kCustom, calls=%fused_computation | custom fusion | bytes 33555456 | tf_op jit(solution)/shard_map/gather | solution.py:20
  136.6 12.5 %fusion.12 = f32[16,128,256,1]{2,1,3,0:T(8,128)} fusion(bf16[16,16,128,128]{2,3,1,0:T(8,128)(2,1)} %broadcast_multiply_fusion, bf16[16,16,128,256]{3,2,1,0:T(8,128)(2,1)} %bitcast.38), kind=kOutput, calls=%fused_computation.29 | convolution fusion | flops 2147483648 | bytes 27262976 | tf_op jit(solution)/shard_map/tkab,tkbf->taf/dot_general | solution.py:21
  149.2 35.3 %reduce-scatter.3.cloned.1.call-done = f32[256,256]{1,0:T(8,128)} async-done(((f32[2048,256]{1,0:T(8,128)}), f32[256,256]{1,0:T(8,128)}) %reduce-scatter.3.cloned.1.call-update) | async-done | bytes 262160 | tf_op jit(solution)/shard_map/reduce_scatter | solution.py:25
  184.6 1.9 multiply_convert_fusion.1
  187.4 2.0 fusion.10
  189.5 34.5 %all-gather.5.cloned.1.call-done = bf16[2048,256]{1,0:T(8,128)(2,1)} async-done(((bf16[256,256]{1,0:T(8,128)(2,1)}), bf16[2048,256]{1,0:T(8,128)(2,1)}) %all-gather.5.cloned.1.call-update) | async-done | bytes 1048592 | tf_op jit(solution)/shard_map/all_gather | solution.py:40
  224.0 4.3 broadcast_in_dim.5
  228.3 108.5 %while.10 = (s32[]{:T(128)}, f32[64,128,256]{2,1,0:T(8,128)}, s32[16,16]{1,0:T(8,128)}, bf16[16,16,128,128]{2,3,1,0:T(8,128)(2,1)}, bf16[16,128,256]{2,1,0:T(8,128)(2,1)}, /*index=5*/s32[]{:T(128)}) while((s32[]{:T(128)}, f32[64,128,256]{2,1,0:T(8,128)}, s32[16,16]{1,0:T(8,128)}, bf16[16,16,128,128]{2,3,1,0:T(8,128)(2,1)}, ...), condition=%wide.region_3.4_spmd, body=%wide.region_1.3_spmd.sunk | while | flops 134742064 | bytes 8979721 | solution.py:53
  228.3 1.5 fusion.26
  230.5 4.6 scatter_fusion
  237.2 4.6 scatter_fusion
  244.0 4.6 scatter_fusion
  250.7 4.7 scatter_fusion
  257.5 4.6 scatter_fusion
  264.3 4.6 scatter_fusion
  271.1 4.7 scatter_fusion
  277.9 4.6 scatter_fusion
  284.7 4.6 scatter_fusion
  291.5 4.6 scatter_fusion
  298.3 4.6 scatter_fusion
  305.1 4.6 scatter_fusion
  311.9 4.6 scatter_fusion
  318.6 4.6 scatter_fusion
  325.4 4.6 scatter_fusion
  332.1 4.6 scatter_fusion
  336.8 145.7 %all-reduce.2.cloned.1.call-done = f32[256,256]{1,0:T(8,128)} async-done(((f32[256,256]{1,0:T(8,128)}), f32[256,256]{1,0:T(8,128)}) %all-reduce.2.cloned.1.call-update) | async-done | bytes 262160 | tf_op jit(solution)/shard_map/psum | solution.py:60
  483.8 386.4 %reduce-scatter.5.cloned.1.call-done = f32[256,256]{1,0:T(8,128)} async-done(((f32[8192,256]{1,0:T(8,128)}), f32[256,256]{1,0:T(8,128)}) %reduce-scatter.5.cloned.1.call-update) | async-done | bytes 262160 | tf_op jit(solution)/shard_map/reduce_scatter | solution.py:54
  870.2 1.7 multiply_convert_fusion
  (54 shorter events, 37.0 us)
Async XLA Ops:
  7.2 177.4 %copy-start = (bf16[256,256]{1,0:T(8,128)(2,1)S(1)}, bf16[256,256]{1,0:T(8,128)(2,1)}, u32[]{:S(2)}) copy-start(bf16[256,256]{1,0:T(8,128)(2,1)} %param.10) | copy-start | bytes 393220
  7.2 117.5 %all-gather.3.cloned.1.call-start = ((), (), s32[]{:S(2)}) async-start(), calls=%async_computation.2 | async-start | bytes 4325376 | tf_op jit(solution)/shard_map/all_gather | solution.py:16
  9.6 174.9 %reduce-scatter.3.cloned.1.call-start = ((), (), s32[]{:S(2)}) async-start(), calls=%async_computation.3 | async-start | bytes 2359296 | tf_op jit(solution)/shard_map/reduce_scatter | solution.py:25
  10.5 12.4 %copy-start.1 = (s32[16]{0:T(128)S(1)}, s32[16]{0:T(128)}, u32[]{:S(2)}) copy-start(s32[16]{0:T(128)} %param.14) | copy-start | bytes 196
  136.6 47.9 %copy-start.2 = (bf16[256,256]{1,0:T(8,128)(2,1)S(1)}, bf16[256,256]{1,0:T(8,128)(2,1)}, u32[]{:S(2)}) copy-start(bf16[256,256]{1,0:T(8,128)(2,1)} %param.12) | copy-start | bytes 393220
  149.2 74.8 %all-gather.5.cloned.1.call-start = ((), (), s32[]{:S(2)}) async-start(), calls=%async_computation.4 | async-start | bytes 1179648 | tf_op jit(solution)/shard_map/all_gather | solution.py:40
  187.4 295.1 %all-reduce.2.cloned.1.call-start = ((), (), s32[]{:S(2)}) async-start(), calls=%async_computation.6 | async-start | bytes 524288 | tf_op jit(solution)/shard_map/psum | solution.py:60
  189.4 680.8 %reduce-scatter.5.cloned.1.call-start = ((), (), s32[]{:S(2)}) async-start(), calls=%async_computation.5 | async-start | bytes 8650752 | tf_op jit(solution)/shard_map/reduce_scatter | solution.py:54
Sparse Core Ops, SparseCore 0:
  12.0 112.6 all-gather.2
  149.3 35.2 reduce-scatter.2
  187.5 36.4 all-gather.4
  229.3 253.1 all-reduce.1
  484.9 385.2 reduce-scatter.4
where the time goes:
time: 880 us; the launch traced here: 878 us
  waiting for transfers between devices  697 us (79%)
  other arithmetic  98.5 us (11%)
  matrix products  40.5 us (5%)
  local copies, waits for them, and re-layouts  28.7 us (3%)
  between operations  13.8 us (2%)
    reduce_scatter x1, waiting for transfers between devices, on_device(): lax.psum_scatter(col_sums.reshape(-1, feat_width), 'row', scatter_dimensi...  386 us
    psum x1, waiting for transfers between devices, on_device(): weight_all = lax.psum(weight_local, ('row', 'rep'))  146 us
    all_gather x1, waiting for transfers between devices, on_device(): gathered = lax.all_gather(scaled_feats, 'row', axis=0, tiled=True)  94.5 us
    scatter-add x16, other arithmetic, add_row(): return (running.at[row_cols].add(contrib), None)  73.9 us
    reduce_scatter x1, waiting for transfers between devices, on_device(): lax.psum_scatter(partial_value, 'rep', scatter_dimension=0, tiled=True)  35.3 us
    all_gather x1, waiting for transfers between devices, on_device(): lax.all_gather(back_rows, 'rep', axis=0, tiled=True)  34.5 us
    dot_general x16, matrix products, add_row(): jnp.einsum('kab,af->kbf', row_pattern, row_back, preferred_element_type=j...  23.3 us
  transfers between devices with their start and end apart: 5, of which 5 were waited for; matrix products, arithmetic and copies ran while one was open for 16% of the time, Pallas kernels for 0%

commit v1 on v0

--- a/solution.py
+++ b/solution.py
@@ -3,25 +3,106 @@
 import jax
 import jax.numpy as jnp
 from jax import lax
+from jax.experimental import pallas as pl
+from jax.experimental.pallas import tpu as pltpu
 from jax.sharding import PartitionSpec as P
+
+
+GROUP = 4
+
+
+def live_tiles(tiles_ref, first, count):
+    picked = [tiles_ref[0, first]]
+    for slot in range(first + 1, first + GROUP):
+        tile = tiles_ref[0, slot]
+        picked.append(jnp.where(slot < count, tile, jnp.zeros_like(tile)))
+    return jnp.concatenate(picked, axis=1)
+
+
+def forward_kernel(cols_ref, len_ref, tiles_ref, section_ref, out_ref):
+    row = pl.program_id(0)
+    count = len_ref[row]
+    out_ref[...] = jnp.zeros_like(out_ref)
+    for first in range(0, tiles_ref.shape[1], GROUP):
+
+        @pl.when(first < count)
+        def _(first=first):
+            picked = jnp.concatenate(
+                [section_ref[cols_ref[row, first + step]] for step in range(GROUP)], axis=0
+            )
+            out_ref[...] += jnp.dot(
+                live_tiles(tiles_ref, first, count),
+                picked,
+                preferred_element_type=jnp.float32,
+            )
+
+
+def backward_kernel(cols_ref, len_ref, tiles_ref, back_ref, out_ref):
+    row = pl.program_id(0)
+    count = len_ref[row]
+    tile = tiles_ref.shape[2]
+
+    @pl.when(row == 0)
+    def _():
+        out_ref[...] = jnp.zeros_like(out_ref)
+
+    for first in range(0, tiles_ref.shape[1], GROUP):
+
+        @pl.when(first < count)
+        def _(first=first):
+            contrib = lax.dot_general(
+                live_tiles(tiles_ref, first, count),
+                back_ref[...],
+                (((0,), (0,)), ((), ())),
+                preferred_element_type=jnp.float32,
+            )
+            for step in range(GROUP):
+                col = cols_ref[row, first + step]
+                out_ref[col] += contrib[step * tile : (step + 1) * tile]
+
+
+def spmm(kernel, tile_cols, list_len, tiles, dense, dense_spec, out_shape, out_spec):
+    rows, slots, tile, _ = tiles.shape
+    width = dense.shape[-1]
+    return pl.pallas_call(
+        kernel,
+        out_shape=out_shape,
+        grid_spec=pltpu.PrefetchScalarGridSpec(
+            num_scalar_prefetch=2,
+            grid=(rows,),
+            in_specs=[
+                pl.BlockSpec((1, slots, tile, tile), lambda i, *_: (i, 0, 0, 0)),
+                dense_spec,
+            ],
+            out_specs=out_spec,
+        ),
+        cost_estimate=pl.CostEstimate(
+            flops=2 * rows * slots * tile * tile * width,
+            bytes_accessed=2 * tiles.size + 2 * dense.size + 4 * math.prod(out_shape.shape),
+            transcendentals=0,
+        ),
+    )(tile_cols, list_len, tiles, dense)
 
 
 def on_device(features, weight, degrees, cotangent, tile_cols, list_len, tiles):
     node_rows, feat_width = features.shape
     tile_rows = tiles.shape[0]
-    slot_count = tiles.shape[1]
     tile_size = tiles.shape[2]
     inv_root = 1.0 / jnp.sqrt(degrees.astype(jnp.float32))
     scaled_feats = (features.astype(jnp.float32) * inv_root[:, None]).astype(jnp.bfloat16)
     gathered = lax.all_gather(scaled_feats, "row", axis=0, tiled=True)
     section_tiles = gathered.reshape(-1, tile_size, feat_width)
-    live_slots = (jnp.arange(slot_count)[None, :] < list_len[:, None]).astype(jnp.bfloat16)
-    pattern = tiles * live_slots[:, :, None, None]
-    picked = section_tiles[tile_cols]
-    partial_value = jnp.einsum(
-        "tkab,tkbf->taf", pattern, picked, preferred_element_type=jnp.float32
+    col_tiles = section_tiles.shape[0]
+    partial_value = spmm(
+        forward_kernel,
+        tile_cols,
+        list_len,
+        tiles,
+        section_tiles,
+        pl.BlockSpec(section_tiles.shape, lambda i, *_: (0, 0, 0)),
+        jax.ShapeDtypeStruct((tile_rows * tile_size, feat_width), jnp.float32),
+        pl.BlockSpec((tile_size, feat_width), lambda i, *_: (i, 0)),
     )
-    partial_value = partial_value.reshape(tile_rows * tile_size, feat_width)
     summed = lax.psum_scatter(partial_value, "rep", scatter_dimension=0, tiled=True)
     pooled = (summed * inv_root[:, None]).astype(jnp.bfloat16)
     preact = jnp.dot(pooled, weight, preferred_element_type=jnp.float32)
@@ -37,20 +118,18 @@
         grad_pre, weight, (((1,), (1,)), ((), ())), preferred_element_type=jnp.float32
     )
     back_rows = (back_rows * inv_root[:, None]).astype(jnp.bfloat16)
-    back_block = lax.all_gather(back_rows, "rep", axis=0, tiled=True).reshape(
-        tile_rows, tile_size, feat_width
+    back_block = lax.all_gather(back_rows, "rep", axis=0, tiled=True)
+    col_shape = (col_tiles, tile_size, feat_width)
+    col_sums = spmm(
+        backward_kernel,
+        tile_cols,
+        list_len,
+        tiles,
+        back_block,
+        pl.BlockSpec((tile_size, feat_width), lambda i, *_: (i, 0)),
+        jax.ShapeDtypeStruct(col_shape, jnp.float32),
+        pl.BlockSpec(col_shape, lambda i, *_: (0, 0, 0)),
     )
-    col_tiles = section_tiles.shape[0]
-
-    def add_row(running, step_inputs):
-        row_pattern, row_cols, row_back = step_inputs
-        contrib = jnp.einsum(
-            "kab,af->kbf", row_pattern, row_back, preferred_element_type=jnp.float32
-        )
-        return (running.at[row_cols].add(contrib), None)
-
-    zero_sums = jnp.zeros((col_tiles, tile_size, feat_width), jnp.float32)
-    col_sums, _ = lax.scan(add_row, zero_sums, (pattern, tile_cols, back_block))
     reduced_cols = lax.psum_scatter(
         col_sums.reshape(-1, feat_width), "row", scatter_dimension=0, tiled=True
     )

time: 880 us -> 872 us (level)
  waiting for transfers between devices: 697 us -> 815 us
  other arithmetic: 98.5 us -> 5.38 us
  matrix products: 40.5 us -> 4.77 us
  Pallas kernels: 0 us -> 32.3 us
  local copies, waits for them, and re-layouts: 28.7 us -> 0.01 us
    psum x1, waiting for transfers between devices: 146 us -> 241 us  [on_device(): weight_all = lax.psum(weight_local, ('row', 'rep'))]
    scatter-add x16 -> x0, other arithmetic: 73.9 us -> none  [add_row(): return (running.at[row_cols].add(contrib), None)]
    dot_general x17 -> x0, matrix products: 35.8 us -> none  [the longest x16 23.3 us: add_row(): jnp.einsum('kab,af->kbf', row_pattern, row_back, preferred_element_type=j...]
    pallas_call x0 -> x2, Pallas kernels: none -> 32.3 us  [spmm(): pl.pallas_call(kernel, out_shape=out_shape, grid_spec=pltpu.PrefetchScala...]
    all_gather x1, waiting for transfers between devices: 94.5 us -> 115 us  [on_device(): gathered = lax.all_gather(scaled_feats, 'row', axis=0, tiled=True)]
    unnamed x7 -> x4, local copies, waits for them, and re-layouts: 12.4 us -> 0.01 us
    gather x1 -> x0, local copies, waits for them, and re-layouts: 12 us -> none  [on_device(): picked = section_tiles[tile_cols]]
    select_n x17 -> x0, other arithmetic: 11.9 us -> none  [the longest x16 11.2 us: add_row(): return (running.at[row_cols].add(contrib), None)]
  transfers between devices with their start and end apart: 5 -> 5, of which waited for: 5 -> 5; matrix products, arithmetic and copies ran while one was open for 16% -> 0% of each run, Pallas kernels for 0% -> 2%
where the time goes in v1:
time: 872 us
  waiting for transfers between devices  815 us (93%)
  Pallas kernels  32.3 us (4%)
  between operations  13.8 us (2%)
    reduce_scatter x1, waiting for transfers between devices, on_device(): lax.psum_scatter(col_sums.reshape(-1, feat_width), 'row', scatter_dimensi...  386 us
    psum x1, waiting for transfers between devices, on_device(): weight_all = lax.psum(weight_local, ('row', 'rep'))  241 us
    all_gather x1, waiting for transfers between devices, on_device(): gathered = lax.all_gather(scaled_feats, 'row', axis=0, tiled=True)  115 us
    reduce_scatter x1, waiting for transfers between devices, on_device(): lax.psum_scatter(partial_value, 'rep', scatter_dimension=0, tiled=True)  38.2 us
    all_gather x1, waiting for transfers between devices, on_device(): back_block = lax.all_gather(back_rows, 'rep', axis=0, tiled=True)  34.3 us
    pallas_call x2, Pallas kernels, spmm(): pl.pallas_call(kernel, out_shape=out_shape, grid_spec=pltpu.PrefetchScala...  32.3 us
  transfers between devices with their start and end apart: 5, of which 5 were waited for; matrix products, arithmetic and copies ran while one was open for 0% of the time, Pallas kernels for 2%

profile of v1, /device:TPU:0, one launch (start us, length us, event | category | flops | bytes accessed | tf_op | source)
XLA Modules:
  0.0 871.5 jit_solution(13553212395578049959)
XLA Ops:
  7.2 0.0 copy-start
  7.2 0.0 all-gather.3.cloned.1.call-start
  7.2 0.7 convert_rsqrt_fusion
  7.9 1.7 multiply_convert_fusion.4
  9.6 0.0 all-gather.3.cloned.1.call-update
  9.6 0.0 reduce-scatter.3.cloned.1.call-start
  9.7 115.0 %all-gather.3.cloned.1.call-done = bf16[8192,256]{1,0:T(8,128)(2,1)} async-done(((bf16[256,256]{1,0:T(8,128)(2,1)}), bf16[8192,256]{1,0:T(8,128)(2,1)}) %all-gather.3.cloned.1.call-update) | async-done | bytes 4194320 | tf_op jit(solution)/shard_map/all_gather | solution.py:93
  124.7 0.0 copy-start.1
  124.7 15.0 %shard_map.94 = f32[2048,256]{1,0:T(8,128)} custom-call(s32[16,16]{1,0:T(8,128)} %cols_ref.3, s32[16]{0:T(128)} %len_ref.3, bf16[16,16,128,128]{3,2,1,0:T(8,128)(2,1)} %tiles_ref.3, bf16[64,128,256]{2,1,0:T(8,128)(2,1)} %bitcast.7), custom_call_target="tpu_custom_call" | custom-call | flops 2147483648 | bytes 14680064 | tf_op jit(solution)/shard_map/pallas_call | solution.py:67
  139.7 0.0 reduce-scatter.3.cloned.1.call-update
  139.7 0.0 all-gather.5.cloned.1.call-start
  139.8 38.2 %reduce-scatter.3.cloned.1.call-done = f32[256,256]{1,0:T(8,128)} async-done(((f32[2048,256]{1,0:T(8,128)}), f32[256,256]{1,0:T(8,128)}) %reduce-scatter.3.cloned.1.call-update) | async-done | bytes 262160 | tf_op jit(solution)/shard_map/reduce_scatter | solution.py:106
  177.9 0.0 copy-done
  177.9 0.0 copy-done.1
  177.9 1.9 multiply_convert_fusion.1
  179.9 0.9 fusion
  180.7 0.0 all-gather.5.cloned.1.call-update
  180.8 0.0 all-reduce.2.cloned.1.call-start
  180.8 2.0 fusion.1
  182.8 0.0 all-reduce.2.cloned.1.call-update
  182.8 0.0 reduce-scatter.5.cloned.1.call-start
  182.9 34.3 %all-gather.5.cloned.1.call-done.back_ref = bf16[2048,256]{1,0:T(8,128)(2,1)} async-done(((bf16[256,256]{1,0:T(8,128)(2,1)}), bf16[2048,256]{1,0:T(8,128)(2,1)}) %all-gather.5.cloned.1.call-update) | async-done | bytes 1048592 | tf_op jit(solution)/shard_map/all_gather | solution.py:121
  217.1 17.3 %shard_map.95 = f32[64,128,256]{2,1,0:T(8,128)} custom-call(s32[16,16]{1,0:T(8,128)} %cols_ref.3, s32[16]{0:T(128)} %len_ref.3, bf16[16,16,128,128]{3,2,1,0:T(8,128)(2,1)} %tiles_ref.3, bf16[2048,256]{1,0:T(8,128)(2,1)} %all-gather.5.cloned.1.call-done.back_ref), custom_call_target="tpu_custom_call" | custom-call | flops 2147483648 | bytes 17825792 | tf_op jit(solution)/shard_map/pallas_call | solution.py:67
  234.4 0.0 reduce-scatter.5.cloned.1.call-update
  234.5 241.1 %all-reduce.2.cloned.1.call-done = f32[256,256]{1,0:T(8,128)} async-done(((f32[256,256]{1,0:T(8,128)}), f32[256,256]{1,0:T(8,128)}) %all-reduce.2.cloned.1.call-update) | async-done | bytes 262160 | tf_op jit(solution)/shard_map/psum | solution.py:139
  475.6 1.3 dynamic-slice_multiply_fusion
  476.9 386.4 %reduce-scatter.5.cloned.1.call-done = f32[256,256]{1,0:T(8,128)} async-done(((f32[8192,256]{1,0:T(8,128)}), f32[256,256]{1,0:T(8,128)}) %reduce-scatter.5.cloned.1.call-update) | async-done | bytes 262160 | tf_op jit(solution)/shard_map/reduce_scatter | solution.py:133
  863.3 1.7 multiply_convert_fusion
Async XLA Ops:
  7.2 170.8 %copy-start = (bf16[256,256]{1,0:T(8,128)(2,1)S(1)}, bf16[256,256]{1,0:T(8,128)(2,1)}, u32[]{:S(2)}) copy-start(bf16[256,256]{1,0:T(8,128)(2,1)} %param.8) | copy-start | bytes 393220
  7.2 117.5 %all-gather.3.cloned.1.call-start = ((), (), s32[]{:S(2)}) async-start(), calls=%async_computation.2 | async-start | bytes 4325376 | tf_op jit(solution)/shard_map/all_gather | solution.py:93
  9.6 168.3 %reduce-scatter.3.cloned.1.call-start = ((), (), s32[]{:S(2)}) async-start(), calls=%async_computation.3 | async-start | bytes 2359296 | tf_op jit(solution)/shard_map/reduce_scatter | solution.py:106
  124.7 53.3 %copy-start.1 = (bf16[256,256]{1,0:T(8,128)(2,1)S(1)}, bf16[256,256]{1,0:T(8,128)(2,1)}, u32[]{:S(2)}) copy-start(bf16[256,256]{1,0:T(8,128)(2,1)} %param.10) | copy-start | bytes 393220
  139.7 77.4 %all-gather.5.cloned.1.call-start = ((), (), s32[]{:S(2)}) async-start(), calls=%async_computation.4 | async-start | bytes 1179648 | tf_op jit(solution)/shard_map/all_gather | solution.py:121
  180.8 294.8 %all-reduce.2.cloned.1.call-start = ((), (), s32[]{:S(2)}) async-start(), calls=%async_computation.6 | async-start | bytes 524288 | tf_op jit(solution)/shard_map/psum | solution.py:139
  182.8 680.5 %reduce-scatter.5.cloned.1.call-start = ((), (), s32[]{:S(2)}) async-start(), calls=%async_computation.5 | async-start | bytes 8650752 | tf_op jit(solution)/shard_map/reduce_scatter | solution.py:133
Sparse Core Ops, SparseCore 0:
  12.0 112.6 all-gather.2
  139.8 38.0 reduce-scatter.2
  180.9 36.1 all-gather.4
  222.4 253.1 all-reduce.1
  478.0 385.2 reduce-scatter.4
